TPU v7x, 128 devices: a whole 4x4x4 slice. The times are simulated.
128 devices in a mesh: cent: 4 (over y), rows: 32 (over z, x, core).
Axes of the slice: x: 4, y: 4, z: 4, core: 2. Of those that a mesh axis runs over, the one named last changes fastest.
Arguments:
- embeddings: bfloat16 [32768, 2048], P(('cent', 'rows')), may hold values from -6 to 6
- centroids: bfloat16 [16384, 2048], P(('cent', 'rows')), may hold values from -0.125 to 0.125
- cluster: int32 [32768, 1], P(('cent', 'rows')), may hold values from 0 to 127; in each aligned block of 256 rows (0 to 255, 256 to 511, ...) at most 4 rows name the same one
- noise_salt: int32 [1], replicated, may hold values from 0 to 1048575
Outputs:
- perturbed_max: float32 [32768], P(('cent', 'rows'))
- dedup_score: float32 [32768], P(('cent', 'rows'))
- new_centroids: float32 [128, 2048], P(('cent', 'rows'))
Inputs may be any that keep to these rules, and one draw needn't show every extreme that they name: In every aligned block of 256 rows (the rows of one device) no cluster is named by more than 4 rows, and in some block some cluster by exactly 4; every cluster is named by some row.
All inputs are finite; a program needn't handle non-finite values.
Results may differ from a plain program's by a relative error of at most 0.0003.
Values may be sent and summed in bfloat16 or wider, within the bound.
A program may use at most 128 MiB of HBM per device.

v0:
```python
import math
import jax
import jax.numpy as jnp
from jax import lax
from jax.sharding import PartitionSpec as P

inverse_temp = 3.0
epsilon = 1e-06


def logical_shift(word, amount):
    return lax.shift_right_logical(word, jnp.full(word.shape, amount, jnp.int32))


def gumbel_noise(row_ids, cent_ids, salt_word):
    mixed = row_ids * 1103515245 + cent_ids * 739982445 + salt_word
    mixed = mixed ^ logical_shift(mixed, 16)
    mixed = mixed * 2146121005
    mixed = mixed ^ logical_shift(mixed, 15)
    mixed = mixed * 1759714725
    mixed = mixed ^ logical_shift(mixed, 16)
    low_bits = mixed & 8388607
    uniform = (low_bits.astype(jnp.float32) + 0.5) * (1.0 / 8388608.0)
    return -jnp.log(-jnp.log(uniform))


def cluster_stats(members, valid):
    feature_dim = members.shape[1]
    widened = members.astype(jnp.float32)
    scale = lax.rsqrt(jnp.mean(widened * widened, axis=1) + epsilon)
    gram = lax.dot_general(
        members, members, (((1,), (1,)), ((), ())), preferred_element_type=jnp.float32
    )
    similar = gram * scale[:, None] * scale[None, :] * (1.0 / math.sqrt(feature_dim))
    order = jnp.arange(members.shape[0], dtype=jnp.int32)
    usable = valid[None, :] & (order[:, None] != order[None, :])
    highest = jnp.max(jnp.where(usable, similar, -1e30), axis=1)
    scores = jnp.where(jnp.any(usable, axis=1), highest, 0.0)
    total = jnp.sum(jnp.where(valid[:, None], widened, 0.0), axis=0)
    center = total * lax.rsqrt(jnp.mean(total * total) + epsilon)
    return (scores, center)


def shards(embeddings, centroids, cluster, noise_salt):
    rows_dev, feature_dim = embeddings.shape
    cent_dev = centroids.shape[0]
    cent_count = lax.axis_size("cent")
    rows_count = lax.axis_size("rows")
    devices = cent_count * rows_count
    capacity = max(2, 2 * rows_dev // devices)
    cent_index = lax.axis_index("cent")
    rows_index = lax.axis_index("rows")
    salt_word = noise_salt[0]
    group = lax.all_gather(embeddings, "cent", axis=0, tiled=True)
    position = jnp.arange(cent_count * rows_dev, dtype=jnp.int32)
    group_ids = (position // rows_dev * rows_count + rows_index) * rows_dev + position % rows_dev
    panel_base = cent_index * (rows_count * cent_dev)
    initial = jnp.full((cent_count * rows_dev,), -1e30, jnp.float32)
    piece = lax.all_gather(centroids, "rows", axis=0, tiled=True)
    piece_rows = piece.shape[0]
    block = math.gcd(piece_rows, 512)
    tiles = piece.reshape(piece_rows // block, block, feature_dim)
    offsets = jnp.arange(piece_rows // block, dtype=jnp.int32) * block

    def step(carry, item):
        tile, offset = item
        scores = lax.dot_general(
            group, tile, (((1,), (1,)), ((), ())), preferred_element_type=jnp.float32
        )
        cent_ids = panel_base + offset + jnp.arange(block, dtype=jnp.int32)
        perturbed = inverse_temp * scores + gumbel_noise(
            group_ids[:, None], cent_ids[None, :], salt_word
        )
        return (jnp.maximum(carry, jnp.max(perturbed, axis=1)), None)

    result, unused = lax.scan(step, initial, (tiles, offsets))
    merged = lax.pmax(result, "cent")
    perturbed_max = lax.dynamic_slice_in_dim(merged, cent_index * rows_dev, rows_dev)
    assigned = cluster[:, 0]
    order = jnp.arange(rows_dev, dtype=jnp.int32)
    same = (assigned[:, None] == assigned[None, :]) & (order[None, :] < order[:, None])
    rank = jnp.sum(same.astype(jnp.int32), axis=1)
    slot = assigned * capacity + rank
    outgoing = jnp.zeros((devices * capacity, feature_dim), jnp.bfloat16).at[slot].set(embeddings)
    present = (
        jnp.zeros((devices * capacity,), jnp.bfloat16)
        .at[slot]
        .set(jnp.ones((rows_dev,), jnp.bfloat16))
    )
    received, arrived = (
        lax.all_to_all(
            outgoing.reshape(devices, capacity, feature_dim),
            ("cent", "rows"),
            split_axis=0,
            concat_axis=0,
            tiled=True,
        ),
        lax.all_to_all(
            present.reshape(devices, capacity),
            ("cent", "rows"),
            split_axis=0,
            concat_axis=0,
            tiled=True,
        ),
    )
    members = received.reshape(devices * capacity, feature_dim)
    valid = arrived.reshape(devices * capacity) > 0.5
    scores, center = cluster_stats(members, valid)
    returned = lax.all_to_all(
        scores.reshape(devices, capacity), ("cent", "rows"), split_axis=0, concat_axis=0, tiled=True
    )
    dedup_score = returned.reshape(devices * capacity)[slot]
    return (perturbed_max, dedup_score, center[None, :])


def solution(mesh):
    in_specs = (
        P(("cent", "rows"), None),
        P(("cent", "rows"), None),
        P(("cent", "rows"), None),
        P(),
    )
    out_specs = (P(("cent", "rows")), P(("cent", "rows")), P(("cent", "rows"), None))
    return jax.shard_map(shards, mesh=mesh, in_specs=in_specs, out_specs=out_specs, check_vma=False)
```

profile of v0, /device:TPU:0, one launch (start us, length us, event | category | flops | bytes accessed | tf_op | source)
XLA Modules:
  0.0 242.6 jit_solution(4939791693935059020)
XLA Ops:
  10.3 2.2 scatter_custom_fusion
  13.2 11.1 %all-to-all-start = ((bf16[128,1,4]{2,1,0:T(2,128)(2,1)}), bf16[128,1,4]{2,1,0:T(2,128)(2,1)S(1)}, u32[]{:S(2)}, u32[]{:S(2)}) async-start(bf16[128,1,4]{2,1,0:T(2,128)(2,1)} %all_to_all.17), calls=%async_computation | async-start | bytes 131072 | tf_op jit(solution)/shard_map/all_to_all | solution.py:98
  24.3 3.5 %scatter_custom_fusion.1 = bf16[512,2048]{1,0:T(8,128)(2,1)S(1)} fusion(s32[256]{0:T(256)S(1)} %bitcast.32, bf16[256,2048]{1,0:T(8,128)(2,1)} %param.6, bf16[]{:T(256)} %constant.99.clone.1), kind=kCustom, calls=%fused_computation.50 | custom fusion | bytes 2097664 | tf_op jit(solution)/shard_map/scatter | solution.py:84
  27.9 2.2 reshape.113
  30.1 3.5 %all-to-all-done = bf16[128,1,4]{2,1,0:T(2,128)(2,1)S(1)} async-done(((bf16[128,1,4]{2,1,0:T(2,128)(2,1)}), bf16[128,1,4]{2,1,0:T(2,128)(2,1)S(1)}, u32[]{:S(2)}, u32[]{:S(2)}) %all-to-all-start) | async-done | bytes 1056 | tf_op jit(solution)/shard_map/all_to_all | solution.py:98
  33.6 6.3 %all-to-all-start.1 = ((bf16[128,4,2048]{2,1,0:T(4,128)(2,1)}), bf16[128,4,2048]{2,1,0:T(4,128)(2,1)S(1)}, u32[]{:S(2)}, u32[]{:S(2)}) async-start(bf16[128,4,2048]{2,1,0:T(4,128)(2,1)} %reshape.113), calls=%async_computation.1 | async-start | bytes 4194304 | tf_op jit(solution)/shard_map/all_to_all | solution.py:91
  40.7 32.1 %all-to-all-done.1 = bf16[128,4,2048]{2,1,0:T(4,128)(2,1)S(1)} async-done(((bf16[128,4,2048]{2,1,0:T(4,128)(2,1)}), bf16[128,4,2048]{2,1,0:T(4,128)(2,1)S(1)}, u32[]{:S(2)}, u32[]{:S(2)}) %all-to-all-start.1) | async-done | bytes 2097184 | tf_op jit(solution)/shard_map/all_to_all | solution.py:91
  72.8 2.1 fusion.33
  75.1 2.1 reshape.114
  77.1 3.6 %fusion.37 = f32[512]{0:T(512)S(1)} fusion(bf16[512,2048]{1,0:T(8,128)(2,1)} %reshape.114, f32[512]{0:T(512)S(1)} %rsqrt.18, pred[512]{0:T(512)(128)(4,1)S(1)} %gt.22), kind=kOutput, calls=%fused_computation.49 | convolution fusion | flops 1075576320 | bytes 2101760 | tf_op jit(solution)/shard_map/dot_general | solution.py:31
  81.5 7.2 %all-to-all-start.2 = ((f32[128,1,4]{2,1,0:T(1,128)}), f32[128,1,4]{2,1,0:T(1,128)S(1)}, u32[]{:S(2)}, u32[]{:S(2)}) async-start(f32[128,1,4]{2,1,0:T(1,128)} %bitcast.5), calls=%async_computation.2 | async-start | bytes 131072 | tf_op jit(solution)/shard_map/all_to_all | solution.py:109
  90.6 7.2 %all-to-all-done.2 = f32[128,1,4]{2,1,0:T(1,128)S(1)} async-done(((f32[128,1,4]{2,1,0:T(1,128)}), f32[128,1,4]{2,1,0:T(1,128)S(1)}, u32[]{:S(2)}, u32[]{:S(2)}) %all-to-all-start.2) | async-done | bytes 2080 | tf_op jit(solution)/shard_map/all_to_all | solution.py:109
  99.3 2.5 %gather_fusion = f32[256]{0:T(256)} fusion(f32[512]{0:T(512)S(1)} %reshape.115, s32[1024]{0:T(1024)S(1)} %pad_clamp_fusion), kind=kCustom, calls=%fused_computation | custom fusion | bytes 3072 | tf_op jit(solution)/shard_map/gather | solution.py:112
  101.8 57.1 %all-gather.3.cloned.1.call-done = bf16[4096,2048]{1,0:T(8,128)(2,1)} async-done(((bf16[128,2048]{1,0:T(8,128)(2,1)}), bf16[4096,2048]{1,0:T(8,128)(2,1)}) %all-gather.3.cloned.1.call-update) | async-done | bytes 16777232 | tf_op jit(solution)/shard_map/all_gather | solution.py:59
  158.8 65.8 %while.11 = (s32[]{:T(128)}, f32[1024]{0:T(1024)S(1)}, bf16[8,512,2048]{2,1,0:T(8,128)(2,1)}, bf16[1024,2048]{1,0:T(8,128)(2,1)}, s32[8]{0:T(128)S(1)}, /*index=...) while((s32[]{:T(128)}, f32[1024]{0:T(1024)S(1)}, bf16[8,512,2048]{2,1,0:T(8,128)(2,1)}, ...), condition=%wide.region_2.3_spmd.clone, body=%wide.region_0.2_spmd.clone.sunk | while | flops 2157464576 | bytes 6320795 | solution.py:76
  160.1 6.9 %fusion.56 = f32[1024]{0:T(1024)S(1)} fusion(bf16[1024,2048]{1,0:T(8,128)(2,1)} %get-tuple-element.168, bf16[8,512,2048]{2,1,0:T(8,128)(2,1)} %get-tuple-element.167, s32[]{:T(128)S(6)} %copy.19, s32[]{:T(128)} %get-tuple-element.171, s32[512]{0:T(512)S(1)} %add_multiply_fusion.2, s32[1024]{0:T(1024)S(1)} %fusion.55), kind=kOutput, calls=%fused_computation.21.clone.1 | convolution fusion | flops 2157444096 | bytes 6302212 | tf_op jit(solution)/shard_map/while/body/eval_jaxpr/dot_general | solution.py:67
  168.3 6.9 %fusion.56 = f32[1024]{0:T(1024)S(1)} fusion(bf16[1024,2048]{1,0:T(8,128)(2,1)} %get-tuple-element.168, bf16[8,512,2048]{2,1,0:T(8,128)(2,1)} %get-tuple-element.167, s32[]{:T(128)S(6)} %copy.19, s32[]{:T(128)} %get-tuple-element.171, s32[512]{0:T(512)S(1)} %add_multiply_fusion.2, s32[1024]{0:T(1024)S(1)} %fusion.55), kind=kOutput, calls=%fused_computation.21.clone.1 | convolution fusion | flops 2157444096 | bytes 6302212 | tf_op jit(solution)/shard_map/while/body/eval_jaxpr/dot_general | solution.py:67
  176.5 6.9 %fusion.56 = f32[1024]{0:T(1024)S(1)} fusion(bf16[1024,2048]{1,0:T(8,128)(2,1)} %get-tuple-element.168, bf16[8,512,2048]{2,1,0:T(8,128)(2,1)} %get-tuple-element.167, s32[]{:T(128)S(6)} %copy.19, s32[]{:T(128)} %get-tuple-element.171, s32[512]{0:T(512)S(1)} %add_multiply_fusion.2, s32[1024]{0:T(1024)S(1)} %fusion.55), kind=kOutput, calls=%fused_computation.21.clone.1 | convolution fusion | flops 2157444096 | bytes 6302212 | tf_op jit(solution)/shard_map/while/body/eval_jaxpr/dot_general | solution.py:67
  184.8 6.9 %fusion.56 = f32[1024]{0:T(1024)S(1)} fusion(bf16[1024,2048]{1,0:T(8,128)(2,1)} %get-tuple-element.168, bf16[8,512,2048]{2,1,0:T(8,128)(2,1)} %get-tuple-element.167, s32[]{:T(128)S(6)} %copy.19, s32[]{:T(128)} %get-tuple-element.171, s32[512]{0:T(512)S(1)} %add_multiply_fusion.2, s32[1024]{0:T(1024)S(1)} %fusion.55), kind=kOutput, calls=%fused_computation.21.clone.1 | convolution fusion | flops 2157444096 | bytes 6302212 | tf_op jit(solution)/shard_map/while/body/eval_jaxpr/dot_general | solution.py:67
  193.0 6.9 %fusion.56 = f32[1024]{0:T(1024)S(1)} fusion(bf16[1024,2048]{1,0:T(8,128)(2,1)} %get-tuple-element.168, bf16[8,512,2048]{2,1,0:T(8,128)(2,1)} %get-tuple-element.167, s32[]{:T(128)S(6)} %copy.19, s32[]{:T(128)} %get-tuple-element.171, s32[512]{0:T(512)S(1)} %add_multiply_fusion.2, s32[1024]{0:T(1024)S(1)} %fusion.55), kind=kOutput, calls=%fused_computation.21.clone.1 | convolution fusion | flops 2157444096 | bytes 6302212 | tf_op jit(solution)/shard_map/while/body/eval_jaxpr/dot_general | solution.py:67
  201.2 6.9 %fusion.56 = f32[1024]{0:T(1024)S(1)} fusion(bf16[1024,2048]{1,0:T(8,128)(2,1)} %get-tuple-element.168, bf16[8,512,2048]{2,1,0:T(8,128)(2,1)} %get-tuple-element.167, s32[]{:T(128)S(6)} %copy.19, s32[]{:T(128)} %get-tuple-element.171, s32[512]{0:T(512)S(1)} %add_multiply_fusion.2, s32[1024]{0:T(1024)S(1)} %fusion.55), kind=kOutput, calls=%fused_computation.21.clone.1 | convolution fusion | flops 2157444096 | bytes 6302212 | tf_op jit(solution)/shard_map/while/body/eval_jaxpr/dot_general | solution.py:67
  209.4 6.9 %fusion.56 = f32[1024]{0:T(1024)S(1)} fusion(bf16[1024,2048]{1,0:T(8,128)(2,1)} %get-tuple-element.168, bf16[8,512,2048]{2,1,0:T(8,128)(2,1)} %get-tuple-element.167, s32[]{:T(128)S(6)} %copy.19, s32[]{:T(128)} %get-tuple-element.171, s32[512]{0:T(512)S(1)} %add_multiply_fusion.2, s32[1024]{0:T(1024)S(1)} %fusion.55), kind=kOutput, calls=%fused_computation.21.clone.1 | convolution fusion | flops 2157444096 | bytes 6302212 | tf_op jit(solution)/shard_map/while/body/eval_jaxpr/dot_general | solution.py:67
  217.7 6.9 %fusion.56 = f32[1024]{0:T(1024)S(1)} fusion(bf16[1024,2048]{1,0:T(8,128)(2,1)} %get-tuple-element.168, bf16[8,512,2048]{2,1,0:T(8,128)(2,1)} %get-tuple-element.167, s32[]{:T(128)S(6)} %copy.19, s32[]{:T(128)} %get-tuple-element.171, s32[512]{0:T(512)S(1)} %add_multiply_fusion.2, s32[1024]{0:T(1024)S(1)} %fusion.55), kind=kOutput, calls=%fused_computation.21.clone.1 | convolution fusion | flops 2157444096 | bytes 6302212 | tf_op jit(solution)/shard_map/while/body/eval_jaxpr/dot_general | solution.py:67
  224.6 10.5 %pmax.7 = f32[1024]{0:T(1024)S(1)} all-reduce(f32[1024]{0:T(1024)S(1)} %get-tuple-element.45), channel_id=1, replica_groups=mesh['cent'=4,'rows'=32] {'cent'}, use_global_device_ids=true, to_apply=%region_3.4 | all-reduce | flops 1024 | bytes 8192 | tf_op jit(solution)/shard_map/pmax | solution.py:77
  (59 shorter events, 13.9 us)
Async XLA Ops:
  7.2 94.6 %all-gather.5.cloned.1.call-start = ((), (), s32[]{:S(2)}) async-start(), calls=%async_computation.4 | async-start | bytes 5242880 | tf_op jit(solution)/shard_map/all_gather | solution.py:54
  7.9 150.9 %all-gather.3.cloned.1.call-start = ((), (), s32[]{:S(2)}) async-start(), calls=%async_computation.3 | async-start | bytes 17301504 | tf_op jit(solution)/shard_map/all_gather | solution.py:59
  13.2 20.4 %all-to-all-start = ((bf16[128,1,4]{2,1,0:T(2,128)(2,1)}), bf16[128,1,4]{2,1,0:T(2,128)(2,1)S(1)}, u32[]{:S(2)}, u32[]{:S(2)}) async-start(bf16[128,1,4]{2,1,0:T(2,128)(2,1)} %all_to_all.17), calls=%async_computation | async-start | bytes 131072 | tf_op jit(solution)/shard_map/all_to_all | solution.py:98
  33.6 39.2 %all-to-all-start.1 = ((bf16[128,4,2048]{2,1,0:T(4,128)(2,1)}), bf16[128,4,2048]{2,1,0:T(4,128)(2,1)S(1)}, u32[]{:S(2)}, u32[]{:S(2)}) async-start(bf16[128,4,2048]{2,1,0:T(4,128)(2,1)} %reshape.113), calls=%async_computation.1 | async-start | bytes 4194304 | tf_op jit(solution)/shard_map/all_to_all | solution.py:91
  81.5 16.3 %all-to-all-start.2 = ((f32[128,1,4]{2,1,0:T(1,128)}), f32[128,1,4]{2,1,0:T(1,128)S(1)}, u32[]{:S(2)}, u32[]{:S(2)}) async-start(f32[128,1,4]{2,1,0:T(1,128)} %bitcast.5), calls=%async_computation.2 | async-start | bytes 131072 | tf_op jit(solution)/shard_map/all_to_all | solution.py:109
Sparse Core Ops, SparseCore 0:
  9.7 73.9 all-gather.4
  85.9 72.9 all-gather.2
where the time goes:
time: 243 us
  waiting for transfers between devices  101 us (42%)
  matrix products  59 us (24%)
  starting transfers between devices  24.7 us (10%)
  local copies, waits for them, and re-layouts  20.6 us (8%)
  between operations  14.9 us (6%)
  blocking collectives  10.5 us (4%)
  other arithmetic  6.36 us (3%)
  loops' own time  5.28 us (2%)
    all_gather x1, waiting for transfers between devices, shards(): piece = lax.all_gather(centroids, 'rows', axis=0, tiled=True)  57.1 us
    dot_general x8, matrix products, step(): lax.dot_general(group, tile, (((1,), (1,)), ((), ())), preferred_element_...  55.4 us
    all_to_all x1, waiting for transfers between devices, shards(): lax.all_to_all(outgoing.reshape(devices, capacity, feature_dim), ('cent',...  32.1 us
    all_to_all x1, starting transfers between devices, shards(): lax.all_to_all(present.reshape(devices, capacity), ('cent', 'rows'), spli...  11.1 us
    pmax x1, blocking collectives, shards(): merged = lax.pmax(result, 'cent')  10.5 us
    all_to_all x1, waiting for transfers between devices, shards(): lax.all_to_all(scores.reshape(devices, capacity), ('cent', 'rows'), split...  7.23 us
    all_to_all x1, starting transfers between devices, shards(): lax.all_to_all(scores.reshape(devices, capacity), ('cent', 'rows'), split...  7.22 us
    all_to_all x1, starting transfers between devices, shards(): lax.all_to_all(outgoing.reshape(devices, capacity, feature_dim), ('cent',...  6.27 us
  transfers between devices with their start and end apart: 5, of which 4 were waited for; matrix products, arithmetic and copies ran while one was open for 10% of the time, Pallas kernels for 0%

commit v1 on v0

--- a/solution.py
+++ b/solution.py
@@ -56,7 +56,8 @@
     group_ids = (position // rows_dev * rows_count + rows_index) * rows_dev + position % rows_dev
     panel_base = cent_index * (rows_count * cent_dev)
     initial = jnp.full((cent_count * rows_dev,), -1e30, jnp.float32)
-    piece = lax.all_gather(centroids, "rows", axis=0, tiled=True)
+    copies = jnp.concatenate([centroids] * lax.axis_size("rows"), axis=0)
+    piece = lax.all_to_all(copies, "rows", 0, 0, tiled=True)
     piece_rows = piece.shape[0]
     block = math.gcd(piece_rows, 512)
     tiles = piece.reshape(piece_rows // block, block, feature_dim)

time: 243 us -> 429 us (1.77)
  waiting for transfers between devices: 101 us -> 238 us
  local copies, waits for them, and re-layouts: 20.6 us -> 64.2 us
  starting transfers between devices: 24.7 us -> 30.9 us
    all_to_all x0 -> x1, waiting for transfers between devices: none -> 163 us  [shards(): piece = lax.all_to_all(copies, 'rows', 0, 0, tiled=True)]
    all_gather x1 -> x0, waiting for transfers between devices: 57.1 us -> none  [shards(): piece = lax.all_gather(centroids, 'rows', axis=0, tiled=True)]
    all_gather x1, waiting for transfers between devices: 0.01 us -> 43.5 us  [shards(): group = lax.all_gather(embeddings, 'cent', axis=0, tiled=True)]
    unnamed x0 -> x33, local copies, waits for them, and re-layouts: none -> 43 us
    all_to_all x1, waiting for transfers between devices: 32.1 us -> 22.8 us  [shards(): lax.all_to_all(outgoing.reshape(devices, capacity, feature_dim), ('cent',...]
    all_to_all x0 -> x1, starting transfers between devices: none -> 5.35 us  [shards(): piece = lax.all_to_all(copies, 'rows', 0, 0, tiled=True)]
  transfers between devices with their start and end apart: 5 -> 5, of which waited for: 4 -> 4; matrix products, arithmetic and copies ran while one was open for 10% -> 13% of each run, Pallas kernels for 0% -> 0%
where the time goes in v1:
time: 429 us; the launch traced here: 427 us
  waiting for transfers between devices  238 us (55%)
  local copies, waits for them, and re-layouts  64.2 us (15%)
  matrix products  59 us (14%)
  starting transfers between devices  30.9 us (7%)
  between operations  14.9 us (3%)
  blocking collectives  8.8 us (2%)
  other arithmetic  6.35 us (1%)
  loops' own time  4.89 us (1%)
    all_to_all x1, waiting for transfers between devices, shards(): piece = lax.all_to_all(copies, 'rows', 0, 0, tiled=True)  163 us
    dot_general x8, matrix products, step(): lax.dot_general(group, tile, (((1,), (1,)), ((), ())), preferred_element_...  55.4 us
    all_gather x1, waiting for transfers between devices, shards(): group = lax.all_gather(embeddings, 'cent', axis=0, tiled=True)  43.5 us
    unnamed x33, local copies, waits for them, and re-layouts  43 us
    all_to_all x1, waiting for transfers between devices, shards(): lax.all_to_all(outgoing.reshape(devices, capacity, feature_dim), ('cent',...  22.8 us
    all_to_all x1, starting transfers between devices, shards(): lax.all_to_all(present.reshape(devices, capacity), ('cent', 'rows'), spli...  11.1 us
    all_to_all x1, starting transfers between devices, shards(): lax.all_to_all(outgoing.reshape(devices, capacity, feature_dim), ('cent',...  9.76 us
    pmax x1, blocking collectives, shards(): merged = lax.pmax(result, 'cent')  8.8 us
  transfers between devices with their start and end apart: 5, of which 4 were waited for; matrix products, arithmetic and copies ran while one was open for 13% of the time, Pallas kernels for 0%

profile of v1, /device:TPU:0, one launch (start us, length us, event | category | flops | bytes accessed | tf_op | source)
XLA Modules:
  0.0 427.5 jit_solution(4961090898855214425)
XLA Ops:
  8.8 2.2 scatter_custom_fusion
  11.7 11.1 %all-to-all-start.1 = ((bf16[128,1,4]{2,1,0:T(2,128)(2,1)}), bf16[128,1,4]{2,1,0:T(2,128)(2,1)S(1)}, u32[]{:S(2)}, u32[]{:S(2)}) async-start(bf16[128,1,4]{2,1,0:T(2,128)(2,1)} %all_to_all.25), calls=%async_computation.1 | async-start | bytes 131072 | tf_op jit(solution)/shard_map/all_to_all | solution.py:99
  59.2 3.5 scatter_custom_fusion.1
  62.7 2.2 reshape.116
  64.9 9.8 %all-to-all-start.2 = ((bf16[128,4,2048]{2,1,0:T(4,128)(2,1)}), bf16[128,4,2048]{2,1,0:T(4,128)(2,1)S(1)}, u32[]{:S(2)}, u32[]{:S(2)}) async-start(bf16[128,4,2048]{2,1,0:T(4,128)(2,1)} %reshape.116), calls=%async_computation.2 | async-start | bytes 4194304 | tf_op jit(solution)/shard_map/all_to_all | solution.py:92
  82.2 22.8 %all-to-all-done.2 = bf16[128,4,2048]{2,1,0:T(4,128)(2,1)S(1)} async-done(((bf16[128,4,2048]{2,1,0:T(4,128)(2,1)}), bf16[128,4,2048]{2,1,0:T(4,128)(2,1)S(1)}, u32[]{:S(2)}, u32[]{:S(2)}) %all-to-all-start.2) | async-done | bytes 2097184 | tf_op jit(solution)/shard_map/all_to_all | solution.py:92
  105.1 2.1 fusion.33
  109.4 3.6 fusion.37
  113.7 4.6 %all-to-all-start.3 = ((f32[128,1,4]{2,1,0:T(1,128)}), f32[128,1,4]{2,1,0:T(1,128)S(1)}, u32[]{:S(2)}, u32[]{:S(2)}) async-start(f32[128,1,4]{2,1,0:T(1,128)} %bitcast.6), calls=%async_computation.3 | async-start | bytes 131072 | tf_op jit(solution)/shard_map/all_to_all | solution.py:110
  119.2 8.5 %all-to-all-done.3 = f32[128,1,4]{2,1,0:T(1,128)S(1)} async-done(((f32[128,1,4]{2,1,0:T(1,128)}), f32[128,1,4]{2,1,0:T(1,128)S(1)}, u32[]{:S(2)}, u32[]{:S(2)}) %all-to-all-start.3) | async-done | bytes 2080 | tf_op jit(solution)/shard_map/all_to_all | solution.py:110
  127.7 5.3 %all-to-all-start = ((bf16[32,128,2048]{2,1,0:T(8,128)(2,1)}), bf16[32,128,2048]{2,1,0:T(8,128)(2,1)}, u32[]{:S(2)}, u32[]{:S(2)}) async-start(bf16[32,128,2048]{2,1,0:T(8,128)(2,1)} %bitcast), calls=%async_computation | async-start | bytes 33554432 | tf_op jit(solution)/shard_map/all_to_all | solution.py:60
  137.1 2.5 gather_fusion
  139.6 43.5 %all-gather.2.cloned.1.call-done = bf16[1024,2048]{1,0:T(8,128)(2,1)} async-done(((bf16[256,2048]{1,0:T(8,128)(2,1)}), bf16[1024,2048]{1,0:T(8,128)(2,1)}) %all-gather.2.cloned.1.call-update) | async-done | bytes 4194320 | tf_op jit(solution)/shard_map/all_gather | solution.py:54
  183.1 162.9 %all-to-all-done = bf16[32,128,2048]{2,1,0:T(8,128)(2,1)} async-done(((bf16[32,128,2048]{2,1,0:T(8,128)(2,1)}), bf16[32,128,2048]{2,1,0:T(8,128)(2,1)}, u32[]{:S(2)}, u32[]{:S(2)}) %all-to-all-start) | async-done | bytes 16777248 | tf_op jit(solution)/shard_map/all_to_all | solution.py:60
  346.1 65.1 %while.11 = (s32[]{:T(128)}, f32[1024]{0:T(1024)S(1)}, bf16[8,512,2048]{2,1,0:T(8,128)(2,1)}, bf16[1024,2048]{1,0:T(8,128)(2,1)}, s32[8]{0:T(128)S(1)}, /*index=...) while((s32[]{:T(128)}, f32[1024]{0:T(1024)S(1)}, bf16[8,512,2048]{2,1,0:T(8,128)(2,1)}, ...), condition=%wide.region_2.3_spmd.clone, body=%wide.region_0.2_spmd.clone.sunk | while | flops 2157464576 | bytes 6320795 | solution.py:77
  347.2 6.9 %fusion.56 = f32[1024]{0:T(1024)S(1)} fusion(bf16[1024,2048]{1,0:T(8,128)(2,1)} %get-tuple-element.168, bf16[8,512,2048]{2,1,0:T(8,128)(2,1)} %get-tuple-element.167, s32[]{:T(128)S(6)} %copy.50, s32[]{:T(128)} %get-tuple-element.171, s32[512]{0:T(512)S(1)} %add_multiply_fusion.2, s32[1024]{0:T(1024)S(1)} %fusion.55), kind=kOutput, calls=%fused_computation.21.clone.1 | convolution fusion | flops 2157444096 | bytes 6302212 | tf_op jit(solution)/shard_map/while/body/eval_jaxpr/dot_general | solution.py:68
  355.4 6.9 %fusion.56 = f32[1024]{0:T(1024)S(1)} fusion(bf16[1024,2048]{1,0:T(8,128)(2,1)} %get-tuple-element.168, bf16[8,512,2048]{2,1,0:T(8,128)(2,1)} %get-tuple-element.167, s32[]{:T(128)S(6)} %copy.50, s32[]{:T(128)} %get-tuple-element.171, s32[512]{0:T(512)S(1)} %add_multiply_fusion.2, s32[1024]{0:T(1024)S(1)} %fusion.55), kind=kOutput, calls=%fused_computation.21.clone.1 | convolution fusion | flops 2157444096 | bytes 6302212 | tf_op jit(solution)/shard_map/while/body/eval_jaxpr/dot_general | solution.py:68
  363.5 6.9 %fusion.56 = f32[1024]{0:T(1024)S(1)} fusion(bf16[1024,2048]{1,0:T(8,128)(2,1)} %get-tuple-element.168, bf16[8,512,2048]{2,1,0:T(8,128)(2,1)} %get-tuple-element.167, s32[]{:T(128)S(6)} %copy.50, s32[]{:T(128)} %get-tuple-element.171, s32[512]{0:T(512)S(1)} %add_multiply_fusion.2, s32[1024]{0:T(1024)S(1)} %fusion.55), kind=kOutput, calls=%fused_computation.21.clone.1 | convolution fusion | flops 2157444096 | bytes 6302212 | tf_op jit(solution)/shard_map/while/body/eval_jaxpr/dot_general | solution.py:68
  371.7 6.9 %fusion.56 = f32[1024]{0:T(1024)S(1)} fusion(bf16[1024,2048]{1,0:T(8,128)(2,1)} %get-tuple-element.168, bf16[8,512,2048]{2,1,0:T(8,128)(2,1)} %get-tuple-element.167, s32[]{:T(128)S(6)} %copy.50, s32[]{:T(128)} %get-tuple-element.171, s32[512]{0:T(512)S(1)} %add_multiply_fusion.2, s32[1024]{0:T(1024)S(1)} %fusion.55), kind=kOutput, calls=%fused_computation.21.clone.1 | convolution fusion | flops 2157444096 | bytes 6302212 | tf_op jit(solution)/shard_map/while/body/eval_jaxpr/dot_general | solution.py:68
  379.8 6.9 %fusion.56 = f32[1024]{0:T(1024)S(1)} fusion(bf16[1024,2048]{1,0:T(8,128)(2,1)} %get-tuple-element.168, bf16[8,512,2048]{2,1,0:T(8,128)(2,1)} %get-tuple-element.167, s32[]{:T(128)S(6)} %copy.50, s32[]{:T(128)} %get-tuple-element.171, s32[512]{0:T(512)S(1)} %add_multiply_fusion.2, s32[1024]{0:T(1024)S(1)} %fusion.55), kind=kOutput, calls=%fused_computation.21.clone.1 | convolution fusion | flops 2157444096 | bytes 6302212 | tf_op jit(solution)/shard_map/while/body/eval_jaxpr/dot_general | solution.py:68
  387.9 6.9 %fusion.56 = f32[1024]{0:T(1024)S(1)} fusion(bf16[1024,2048]{1,0:T(8,128)(2,1)} %get-tuple-element.168, bf16[8,512,2048]{2,1,0:T(8,128)(2,1)} %get-tuple-element.167, s32[]{:T(128)S(6)} %copy.50, s32[]{:T(128)} %get-tuple-element.171, s32[512]{0:T(512)S(1)} %add_multiply_fusion.2, s32[1024]{0:T(1024)S(1)} %fusion.55), kind=kOutput, calls=%fused_computation.21.clone.1 | convolution fusion | flops 2157444096 | bytes 6302212 | tf_op jit(solution)/shard_map/while/body/eval_jaxpr/dot_general | solution.py:68
  396.1 6.9 %fusion.56 = f32[1024]{0:T(1024)S(1)} fusion(bf16[1024,2048]{1,0:T(8,128)(2,1)} %get-tuple-element.168, bf16[8,512,2048]{2,1,0:T(8,128)(2,1)} %get-tuple-element.167, s32[]{:T(128)S(6)} %copy.50, s32[]{:T(128)} %get-tuple-element.171, s32[512]{0:T(512)S(1)} %add_multiply_fusion.2, s32[1024]{0:T(1024)S(1)} %fusion.55), kind=kOutput, calls=%fused_computation.21.clone.1 | convolution fusion | flops 2157444096 | bytes 6302212 | tf_op jit(solution)/shard_map/while/body/eval_jaxpr/dot_general | solution.py:68
  404.2 6.9 %fusion.56 = f32[1024]{0:T(1024)S(1)} fusion(bf16[1024,2048]{1,0:T(8,128)(2,1)} %get-tuple-element.168, bf16[8,512,2048]{2,1,0:T(8,128)(2,1)} %get-tuple-element.167, s32[]{:T(128)S(6)} %copy.50, s32[]{:T(128)} %get-tuple-element.171, s32[512]{0:T(512)S(1)} %add_multiply_fusion.2, s32[1024]{0:T(1024)S(1)} %fusion.55), kind=kOutput, calls=%fused_computation.21.clone.1 | convolution fusion | flops 2157444096 | bytes 6302212 | tf_op jit(solution)/shard_map/while/body/eval_jaxpr/dot_general | solution.py:68
  411.2 8.8 %pmax.7 = f32[1024]{0:T(1024)S(1)} all-reduce(f32[1024]{0:T(1024)S(1)} %get-tuple-element.45), channel_id=1, replica_groups=mesh['cent'=4,'rows'=32] {'cent'}, use_global_device_ids=true, to_apply=%region_3.4 | all-reduce | flops 1024 | bytes 8192 | tf_op jit(solution)/shard_map/pmax | solution.py:78
  (92 shorter events, 58.8 us)
Async XLA Ops:
  7.2 46.0 %copy-start = (bf16[128,2048]{1,0:T(8,128)(2,1)S(1)}, bf16[128,2048]{1,0:T(8,128)(2,1)}, u32[]{:S(2)}) copy-start(bf16[128,2048]{1,0:T(8,128)(2,1)} %param.7) | copy-start | bytes 1572868
  11.7 53.2 %all-to-all-start.1 = ((bf16[128,1,4]{2,1,0:T(2,128)(2,1)}), bf16[128,1,4]{2,1,0:T(2,128)(2,1)S(1)}, u32[]{:S(2)}, u32[]{:S(2)}) async-start(bf16[128,1,4]{2,1,0:T(2,128)(2,1)} %all_to_all.25), calls=%async_computation.1 | async-start | bytes 131072 | tf_op jit(solution)/shard_map/all_to_all | solution.py:99
  64.9 40.2 %all-to-all-start.2 = ((bf16[128,4,2048]{2,1,0:T(4,128)(2,1)}), bf16[128,4,2048]{2,1,0:T(4,128)(2,1)S(1)}, u32[]{:S(2)}, u32[]{:S(2)}) async-start(bf16[128,4,2048]{2,1,0:T(4,128)(2,1)} %reshape.116), calls=%async_computation.2 | async-start | bytes 4194304 | tf_op jit(solution)/shard_map/all_to_all | solution.py:92
  113.7 13.9 %all-to-all-start.3 = ((f32[128,1,4]{2,1,0:T(1,128)}), f32[128,1,4]{2,1,0:T(1,128)S(1)}, u32[]{:S(2)}, u32[]{:S(2)}) async-start(f32[128,1,4]{2,1,0:T(1,128)} %bitcast.6), calls=%async_computation.3 | async-start | bytes 131072 | tf_op jit(solution)/shard_map/all_to_all | solution.py:110
  127.7 218.4 %all-to-all-start = ((bf16[32,128,2048]{2,1,0:T(8,128)(2,1)}), bf16[32,128,2048]{2,1,0:T(8,128)(2,1)}, u32[]{:S(2)}, u32[]{:S(2)}) async-start(bf16[32,128,2048]{2,1,0:T(8,128)(2,1)} %bitcast), calls=%async_computation | async-start | bytes 33554432 | tf_op jit(solution)/shard_map/all_to_all | solution.py:60
  133.0 50.1 %all-gather.2.cloned.1.call-start = ((), (), s32[]{:S(2)}) async-start(), calls=%async_computation.4 | async-start | bytes 5242880 | tf_op jit(solution)/shard_map/all_gather | solution.py:54
Sparse Core Ops, SparseCore 0:
  135.5 47.5 all-gather.1
